TPU v7x, 32 devices: a whole 2x2x4 slice. The times are simulated.
32 devices in a mesh: seq: 8 (over y, x, core), head: 4 (over z).
Axes of the slice: x: 2, y: 2, z: 4, core: 2. Of those that a mesh axis runs over, the one named last changes fastest.
Arguments:
- queries: bfloat16 [8192, 32, 128], P(('seq', 'head')), may hold values from -6 to 6
- keys: bfloat16 [8192, 32, 2, 128], P(('seq', 'head')), may hold values from -6 to 6
- values: bfloat16 [8192, 32, 2, 128], P(('seq', 'head')), may hold values from -6 to 6
- initial_state: float32 [32, 128, 128], P('head'), may hold values from -192 to 192
Outputs:
- mixed: bfloat16 [8192, 32, 128], P(('seq', 'head'))
All inputs are finite; a program needn't handle non-finite values.
Results may differ from a plain program's by a relative error of at most 0.004.
Values may be sent and summed in bfloat16 or wider, within the bound.
A program may use at most 128 MiB of HBM per device.

v0:
```python
import functools

import jax
import jax.numpy as jnp
from jax import lax
from jax.experimental import pallas as pl
from jax.experimental.pallas import tpu as pltpu
from jax.sharding import PartitionSpec as P

BLOCK = 64
BASE = 16
HEADS_A_STEP = 8
INBOX_BYTES = 24 << 20
VMEM_BYTES = 56 << 20

F32 = jnp.float32
BF16 = jnp.bfloat16
MESH = pl.DeviceIdType.MESH


def mm(left, right, dims=((1,), (0,))):
    return lax.dot_general(left, right, (dims, ((), ())), preferred_element_type=F32)


def split(x):
    high = x.astype(BF16)
    return high, (x - high.astype(F32)).astype(BF16)


def cat(parts, axis):
    return jnp.concatenate(parts, axis=axis)


def exact_left(left, right):
    high, low = split(right)
    return mm(cat([left, left], 1), cat([high, low], 0))


def exact_right(left, right):
    high, low = split(left)
    return mm(cat([high, low], 1), cat([right, right], 0))


def both_split(lh, ll, rh, rl):
    return mm(cat([lh, ll], 1), cat([rh, rh], 0)) + mm(lh, rl)


def both(left, right):
    return both_split(*split(left), *split(right))


def odd_rows(x, size):
    rows = x.shape[0]
    return cat([x[s : s + size] for s in range(size, rows, 2 * size)], 0)


def merge_rows(even_from, odd, size):
    rows = even_from.shape[0]
    parts = []
    for i, s in enumerate(range(0, rows, 2 * size)):
        parts += [even_from[s : s + size], odd[i * size : (i + 1) * size]]
    return cat(parts, 0)


def unit_lower_inverses(xs):
    n = xs[0].shape[0]
    row = lax.broadcasted_iota(jnp.int32, (n, n), 0)
    col = lax.broadcasted_iota(jnp.int32, (n, n), 1)
    same = row // BASE == col // BASE
    sub = lax.broadcasted_iota(jnp.int32, (BASE, n), 0)
    lane = lax.broadcasted_iota(jnp.int32, (BASE, n), 1)
    packs = []
    for x in xs:
        inner = jnp.where(same, x, 0.0)
        packed = inner[:BASE]
        for s in range(BASE, n, BASE):
            packed = packed + inner[s : s + BASE]
        packs.append(packed)
    invs = [jnp.where(sub == lane % BASE, 1.0, 0.0) for _ in xs]
    for j in range(BASE - 1):
        at = lane - lane % BASE + j
        coefs = [jnp.take_along_axis(packed, at, axis=1) for packed in packs]
        invs = [inv - coef * inv[j : j + 1] for inv, coef in zip(invs, coefs)]
    ms = [jnp.where(same, cat([inv] * (n // BASE), 0), 0.0) for inv in invs]
    size = BASE
    while size < n:
        near = col // size == row // size - 1
        belows = [split(odd_rows(jnp.where(near, x, 0.0), size)) for x in xs]
        halves = [split(m) for m in ms]
        ys = [both_split(*below, *half) for below, half in zip(belows, halves)]
        ys = [split(merge_rows(jnp.zeros((n, n), F32), y, size)) for y in ys]
        zs = [
            both_split(odd_rows(mh, size), odd_rows(ml, size), *y)
            for (mh, ml), y in zip(halves, ys)
        ]
        ms = [merge_rows(m, odd_rows(m, size) - z, size) for m, z in zip(ms, zs)]
        size *= 2
    return ms


def block_factors(blocks):
    n, width = blocks[0][1].shape
    tokens = blocks[0][0].shape[0]
    row = lax.broadcasted_iota(jnp.int32, (n, n), 0)
    col = lax.broadcasted_iota(jnp.int32, (n, n), 1)
    trow = lax.broadcasted_iota(jnp.int32, (tokens, n), 0)
    tcol = lax.broadcasted_iota(jnp.int32, (tokens, n), 1)
    visible = tcol < (trow + 1) * (n // tokens)
    kqs = [cat([k, q], 0) for q, k, _ in blocks]
    products = [mm(kq, k, ((1,), (1,))) for kq, (_, k, _) in zip(kqs, blocks)]
    xs, d_cols, d_rows, seens = [], [], [], []
    for gs in products:
        gram = gs[:n]
        diag = jnp.where(row == col, gram, 0.0)
        d_col = lax.rsqrt(jnp.sum(diag, axis=1, keepdims=True) + 1e-06)
        d_row = lax.rsqrt(jnp.sum(diag, axis=0, keepdims=True) + 1e-06)
        xs.append(jnp.where(col < row, (2.0 * d_col) * gram * d_row, 0.0))
        d_cols.append(d_col)
        d_rows.append(d_row)
        seens.append(split(jnp.where(visible, gs[n:], 0.0)))
    scaled = [m * (2.0 * d_col) for m, d_col in zip(unit_lower_inverses(xs), d_cols)]
    feds = [exact_right(m, v) for m, (_, _, v) in zip(scaled, blocks)]
    nears = [split(m * d_row) for m, d_row in zip(scaled, d_rows)]
    return kqs, nears, feds, seens


def local_maps(q_ref, k_ref, v_ref, local_ref, gain_ref, first):
    tokens, heads, width = q_ref.shape
    per_token = k_ref.shape[2]
    step = min(BLOCK, tokens)
    n = step * per_token
    count = tokens // step
    blocks = [
        (
            q_ref[b * step : (b + 1) * step, h],
            k_ref[b * step : (b + 1) * step, h].reshape(n, width),
            v_ref[b * step : (b + 1) * step, h].reshape(n, width),
        )
        for b in range(count)
        for h in range(heads)
    ]
    kqs, nears, feds, seens = block_factors(blocks)
    row = lax.broadcasted_iota(jnp.int32, (width, width), 0)
    col = lax.broadcasted_iota(jnp.int32, (width, width), 1)
    eye = jnp.where(row == col, 1.0, 0.0)
    pairs = [cat([jnp.zeros((width, width), F32), eye], 1)] * heads
    for b in range(count):
        at = slice(b * heads, (b + 1) * heads)
        if b == 0:
            qs = [kq[n:].astype(F32) for kq in kqs[at]]
            passed = [cat([jnp.zeros_like(q), q], 1) for q in qs]
            feeds = [
                cat([fed, -mm(cat(list(near), 1), cat([kq[:n], kq[:n]], 0))], 1)
                for fed, near, kq in zip(feds[at], nears[at], kqs[at])
            ]
        else:
            aheads = [exact_left(kq, pair) for kq, pair in zip(kqs[at], pairs)]
            passed = [ahead[n:] for ahead in aheads]
            feeds = [
                cat([fed, jnp.zeros_like(fed)], 1) - both_split(*near, *split(ahead[:n]))
                for fed, near, ahead in zip(feds[at], nears[at], aheads)
            ]
        feeds = [split(feed) for feed in feeds]
        pairs = [
            pair + mm(cat([kq[:n], kq[:n]], 0), cat(list(feed), 0), ((0,), (0,)))
            for pair, kq, feed in zip(pairs, kqs[at], feeds)
        ]
        outs = [
            base + both_split(*seen, *feed)
            for base, seen, feed in zip(passed, seens[at], feeds)
        ]
        for h, out in enumerate(outs):
            local_ref[first + h, b * step : (b + 1) * step] = out[:, :width]
            gain_ref[first + h, b * step : (b + 1) * step] = out[:, width:]
    return pairs


def group_of(step, ns, nh, size):
    own = (lax.axis_index("head") * ns + lax.axis_index("seq")) // size
    groups = ns * nh // size
    return lax.rem(own + 1 + step, groups)


def mixer_kernel(
    ns,
    nh,
    q_ref,
    k_ref,
    v_ref,
    init_ref,
    out_ref,
    local,
    gain,
    t_out,
    a_out,
    t_box,
    a_box,
    states,
    incoming,
    t_send,
    a_send,
    t_recv,
    a_recv,
    s_send,
    s_recv,
):
    tokens, size, width = q_ref.shape
    step = pl.program_id(0)
    si, zi = lax.axis_index("seq"), lax.axis_index("head")
    me = si * nh + zi
    n = ns * nh
    mine = zi * ns + si

    def place(p):
        return p // nh, lax.rem(p, nh)

    def owner(head):
        return lax.rem(head, ns), head // ns

    def map_copies(head):
        return [
            pltpu.make_async_remote_copy(
                src_ref=src.at[head],
                dst_ref=box.at[me],
                send_sem=send.at[head],
                recv_sem=recv.at[me],
                device_id=owner(head),
                device_id_type=MESH,
            )
            for src, box, send, recv in (
                (t_out, t_box, t_send, t_recv),
                (a_out, a_box, a_send, a_recv),
            )
        ]

    def state_copy(d):
        return pltpu.make_async_remote_copy(
            src_ref=states.at[d],
            dst_ref=incoming.at[mine],
            send_sem=s_send.at[d],
            recv_sem=s_recv.at[mine],
            device_id=place(d),
            device_id_type=MESH,
        )

    @pl.when(step == 0)
    def _():
        barrier = pltpu.get_barrier_semaphore()

        @pl.loop(1, n)
        def _(i):
            pl.semaphore_signal(
                barrier, inc=1, device_id=place(lax.rem(me + i, n)), device_id_type=MESH
            )

        pl.semaphore_wait(barrier, n - 1)

    first = group_of(step, ns, nh, size) * size
    pairs = local_maps(q_ref, k_ref, v_ref, local, gain, first)
    for h, pair in enumerate(pairs):
        t_out[first + h] = pair[:, width:]
        a_out[first + h] = pair[:, :width].astype(a_out.dtype)

    @pl.loop(first, first + size)
    def _(head):
        @pl.when(head != mine)
        def _():
            for copy in map_copies(head):
                copy.start()

        @pl.when(head == mine)
        def _():
            pltpu.make_async_copy(t_out.at[mine], t_box.at[me], t_recv.at[me]).start()
            pltpu.make_async_copy(a_out.at[mine], a_box.at[me], a_recv.at[me]).start()

    @pl.when(step == pl.num_programs(0) - 1)
    def _():
        def advance(d, state):
            states[d] = state.astype(states.dtype)

            @pl.when(d != me)
            def _():
                state_copy(d).start()

            @pl.when(d == me)
            def _():
                pltpu.make_async_copy(
                    states.at[d], incoming.at[mine], s_recv.at[mine]
                ).start()

            pltpu.make_async_copy(t_box.at[d], t_box.at[d], t_recv.at[d]).wait()
            pltpu.make_async_copy(a_box.at[d], a_box.at[d], a_recv.at[d]).wait()
            return both(t_box[d], state) + a_box[d].astype(F32)

        lax.fori_loop(0, n, advance, init_ref[si])

        @pl.loop(0, n // size)
        def _(g):
            heads = [g * size + h for h in range(size)]
            for head in heads:
                pltpu.make_async_copy(
                    incoming.at[head], incoming.at[head], s_recv.at[head]
                ).wait()
            for head in heads:
                raw = local[head] + exact_right(gain[head], incoming[head])
                mean = jnp.mean(raw * raw, axis=-1, keepdims=True)
                out_ref[head] = (raw * lax.rsqrt(mean + 1e-06)).astype(out_ref.dtype)

        @pl.loop(0, n)
        def _(head):
            @pl.when(head != mine)
            def _():
                for copy in map_copies(head):
                    copy.wait_send()

            @pl.when(head != me)
            def _():
                state_copy(head).wait_send()


def mixer(q, k, v, initial_state):
    ns, nh = lax.axis_size("seq"), lax.axis_size("head")
    tokens, heads, width = q.shape
    g = HEADS_A_STEP

    def spec(rows):
        return pl.BlockSpec((g, rows, width), lambda i: (group_of(i, ns, nh, g), 0, 0))

    def by_token(rows):
        return pl.BlockSpec(
            (tokens, g, rows, width), lambda i: (0, group_of(i, ns, nh, g), 0, 0)
        )

    square = (heads, width, width)
    return pl.pallas_call(
        functools.partial(mixer_kernel, ns, nh),
        grid=(heads // g,),
        in_specs=[
            pl.BlockSpec((tokens, g, width), lambda i: (0, group_of(i, ns, nh, g), 0)),
            by_token(k.shape[2]),
            by_token(k.shape[2]),
            pl.BlockSpec(initial_state.shape, lambda i: (0, 0, 0)),
        ],
        out_specs=pl.BlockSpec((heads, tokens, width), lambda i: (0, 0, 0)),
        out_shape=jax.ShapeDtypeStruct((heads, tokens, width), BF16),
        scratch_shapes=[
            pltpu.VMEM((heads, tokens, width), F32),
            pltpu.VMEM((heads, tokens, width), F32),
            pltpu.VMEM(square, F32),
            pltpu.VMEM(square, BF16),
            pltpu.VMEM(square, F32),
            pltpu.VMEM(square, BF16),
            pltpu.VMEM(square, BF16),
            pltpu.VMEM(square, BF16),
        ]
        + [pltpu.SemaphoreType.DMA((heads,))] * 6,
        compiler_params=pltpu.CompilerParams(
            collective_id=0, has_side_effects=True, vmem_limit_bytes=VMEM_BYTES
        ),
        name="mixer",
    )(q, k, v, initial_state)


def owned_per_device(queries, keys, values, initial_state):
    tokens, heads, width = queries.shape
    return jnp.swapaxes(mixer(queries, keys, values, initial_state), 0, 1)


HIGH = lax.Precision.HIGHEST


def shifted(value, axis, by):
    size = lax.axis_size(axis)
    pairs = [(i, i + by) for i in range(size) if 0 <= i + by < size]
    return lax.ppermute(value, axis, pairs)


def matmul(left, right):
    return jnp.dot(left, right, precision=HIGH, preferred_element_type=jnp.float32)


def batched(left, right):
    return jnp.einsum("hij,hjk->hik", left, right, precision=HIGH)


def unit_rows(raw_keys):
    floats = raw_keys.astype(jnp.float32)
    return floats * lax.rsqrt(jnp.sum(floats * floats, axis=-1, keepdims=True) + 1e-06)


def all_factors(k_blocks, v_blocks):
    updates = k_blocks.shape[2]
    head_width = k_blocks.shape[3]
    gram = jnp.einsum("hbid,hbjd->hbij", k_blocks, k_blocks, precision=HIGH)
    system = jnp.eye(updates, dtype=jnp.float32) + jnp.tril(2.0 * gram, -1)
    solved = lax.linalg.triangular_solve(
        system,
        2.0 * jnp.concatenate([k_blocks, v_blocks], axis=-1),
        left_side=True,
        lower=True,
        unit_diagonal=True,
    )
    return (solved[..., :head_width], solved[..., head_width:])


def visible_scores(q_blk, k_blk):
    rows = q_blk.shape[0]
    updates = k_blk.shape[0]
    per_token = updates // rows
    row_ids = lax.broadcasted_iota(jnp.int32, (rows, updates), 0)
    col_ids = lax.broadcasted_iota(jnp.int32, (rows, updates), 1)
    return jnp.where(col_ids < (row_ids + 1) * per_token, matmul(q_blk, k_blk.T), 0.0)


def start_pair(head_width):
    return jnp.concatenate(
        [jnp.zeros((head_width, head_width), jnp.float32), jnp.eye(head_width, dtype=jnp.float32)],
        axis=1,
    )


def carried_pass(q_blocks, k_blocks, w_blocks, u_blocks):
    head_width = q_blocks.shape[2]

    def advance(pair_state, block_item):
        q_blk, k_blk, w_mat, u_mat = block_item
        feed_rows = jnp.concatenate([u_mat, jnp.zeros_like(u_mat)], axis=1) - matmul(
            w_mat, pair_state
        )
        outputs = matmul(q_blk, pair_state) + matmul(visible_scores(q_blk, k_blk), feed_rows)
        return (pair_state + matmul(k_blk.T, feed_rows), outputs)

    final_pair, outputs = lax.scan(
        advance, start_pair(head_width), (q_blocks, k_blocks, w_blocks, u_blocks)
    )
    outputs = outputs.reshape(-1, 2 * head_width)
    return (
        final_pair[:, head_width:],
        final_pair[:, :head_width],
        outputs[:, :head_width],
        outputs[:, head_width:],
    )


def per_device(queries, keys, values, initial_state):
    q_heads, k_heads, v_heads = (
        lax.all_to_all(queries, "head", split_axis=1, concat_axis=0, tiled=True),
        lax.all_to_all(keys, "head", split_axis=1, concat_axis=0, tiled=True),
        lax.all_to_all(values, "head", split_axis=1, concat_axis=0, tiled=True),
    )
    head_width = q_heads.shape[2]
    local_heads = q_heads.shape[1]
    blocks = q_heads.shape[0] // BLOCK
    q_blocks = jnp.moveaxis(q_heads.astype(jnp.float32), 1, 0).reshape(
        local_heads, blocks, BLOCK, head_width
    )
    k_blocks = jnp.moveaxis(unit_rows(k_heads), 1, 0).reshape(local_heads, blocks, -1, head_width)
    v_blocks = jnp.moveaxis(v_heads.astype(jnp.float32), 1, 0).reshape(
        local_heads, blocks, -1, head_width
    )
    w_blocks, u_blocks = all_factors(k_blocks, v_blocks)
    transition, additive, local_out, query_gain = jax.vmap(carried_pass)(
        q_blocks, k_blocks, w_blocks, u_blocks
    )
    at_first = lax.axis_index("seq") == 0
    start_state = jnp.where(at_first, initial_state, jnp.zeros_like(initial_state))

    def relay_step(loop_step, current):
        passed = shifted(batched(transition, current) + additive, "seq", 1)
        return jnp.where(at_first, initial_state, passed)

    incoming = lax.fori_loop(0, lax.axis_size("seq") - 1, relay_step, start_state)
    raw_out = local_out + batched(query_gain, incoming)
    scaled = raw_out * lax.rsqrt(jnp.mean(raw_out * raw_out, axis=-1, keepdims=True) + 1e-06)
    tokens_major = jnp.moveaxis(scaled.astype(jnp.bfloat16), 0, 1)
    return lax.all_to_all(tokens_major, "head", split_axis=0, concat_axis=1, tiled=True)


def solution(mesh):
    placed = (
        P(("seq", "head"), None, None),
        P(("seq", "head"), None, None, None),
        P(("seq", "head"), None, None, None),
        P("head", None, None),
    )
    devices = mesh.shape["seq"] * mesh.shape["head"]

    def chosen(queries, keys, values, initial_state):
        own_heads, width = initial_state.shape[:2]
        inbox = devices * 2 * width * width * 4
        if own_heads == mesh.shape["seq"] and inbox <= INBOX_BYTES:
            return owned_per_device(queries, keys, values, initial_state)
        return per_device(queries, keys, values, initial_state)

    return jax.shard_map(
        chosen,
        mesh=mesh,
        in_specs=placed,
        out_specs=P(("seq", "head"), None, None),
        check_vma=False,
    )
```

profile of v0, /device:TPU:7, one launch (start us, length us, event | category | flops | bytes accessed | tf_op | source)
XLA Modules:
  0.0 131.8 jit_solution(1588352136854416899)
XLA Ops:
  0.0 127.5 %mixer.1 = bf16[32,256,128]{2,1,0:T(8,128)(2,1)} custom-call(bf16[256,32,128]{2,1,0:T(8,128)(2,1)} %q_ref.1, bf16[256,32,2,128]{3,2,1,0:T(2,128)(2,1)} %k_ref.1, bf16[256,32,2,128]{3,2,1,0:T(2,128)(2,1)} %v_ref.1, f32[8,128,128]{2,1,0:T(8,128)} %init_ref.1), custom_call_target="tpu_custom_call" | custom-call | tf_op jit(solution)/shard_map/mixer/pallas_call | solution.py:335
  127.5 4.3 %copy.5 = bf16[256,32,128]{2,1,0:T(8,128)(2,1)} copy(bf16[256,32,128]{2,0,1:T(8,128)(2,1)} %bitcast.1) | data formatting | bytes 4194304 | tf_op jit(solution)/shard_map/transpose | solution.py:366
where the time goes:
time: 132 us
  Pallas kernels  127 us (96%)
  local copies, waits for them, and re-layouts  4.26 us (3%)
    pallas_call x1, Pallas kernels, mixer(): pl.pallas_call(functools.partial(mixer_kernel, ns, nh), grid=(heads // g,...  127 us
    transpose x1, local copies, waits for them, and re-layouts, owned_per_device(): return jnp.swapaxes(mixer(queries, keys, values, initial_state), 0, 1)  4.26 us

commit v1 on v0

--- a/solution.py
+++ b/solution.py
@@ -10,7 +10,7 @@
 BLOCK = 64
 BASE = 16
 HEADS_A_STEP = 8
-INBOX_BYTES = 24 << 20
+UNIT = 4
 VMEM_BYTES = 56 << 20
 
 F32 = jnp.float32
@@ -124,8 +124,9 @@
     return kqs, nears, feds, seens
 
 
-def local_maps(q_ref, k_ref, v_ref, local_ref, gain_ref, first):
-    tokens, heads, width = q_ref.shape
+def local_maps(q_ref, k_ref, v_ref, local_ref, gain_ref, first, picked):
+    tokens, _, width = q_ref.shape
+    heads = len(picked)
     per_token = k_ref.shape[2]
     step = min(BLOCK, tokens)
     n = step * per_token
@@ -137,7 +138,7 @@
             v_ref[b * step : (b + 1) * step, h].reshape(n, width),
         )
         for b in range(count)
-        for h in range(heads)
+        for h in picked
     ]
     kqs, nears, feds, seens = block_factors(blocks)
     row = lax.broadcasted_iota(jnp.int32, (width, width), 0)
@@ -169,16 +170,14 @@
             base + both_split(*seen, *feed)
             for base, seen, feed in zip(passed, seens[at], feeds)
         ]
-        for h, out in enumerate(outs):
+        for h, out in zip(picked, outs):
             local_ref[first + h, b * step : (b + 1) * step] = out[:, :width]
             gain_ref[first + h, b * step : (b + 1) * step] = out[:, width:]
     return pairs
 
 
-def group_of(step, ns, nh, size):
-    own = (lax.axis_index("head") * ns + lax.axis_index("seq")) // size
-    groups = ns * nh // size
-    return lax.rem(own + 1 + step, groups)
+def landed(ref, at, sem):
+    pltpu.make_async_copy(ref.at[at], ref.at[at], sem.at[at]).wait()
 
 
 def mixer_kernel(
@@ -191,57 +190,233 @@
     out_ref,
     local,
     gain,
+    t_own,
+    a_own,
+    t_box,
+    a_box,
     t_out,
     a_out,
-    t_box,
-    a_box,
-    states,
-    incoming,
+    t_line,
+    a_line,
+    s_line,
+    s_in,
+    s_fwd,
+    init_box,
     t_send,
     a_send,
     t_recv,
     a_recv,
+    tl_recv,
+    al_recv,
+    sl_send,
     s_send,
     s_recv,
+    i_send,
+    i_recv,
 ):
-    tokens, size, width = q_ref.shape
+    size, width = q_ref.shape[1], q_ref.shape[2]
+    heads = out_ref.shape[0]
     step = pl.program_id(0)
-    si, zi = lax.axis_index("seq"), lax.axis_index("head")
-    me = si * nh + zi
+    s, z = lax.axis_index("seq"), lax.axis_index("head")
     n = ns * nh
-    mine = zi * ns + si
+    me = s * nh + z
+    way = UNIT // 2
+    ticks = heads // UNIT
+    ends = (0, nh - 1)
+    at_end = (z == 0) | (z == nh - 1)
 
     def place(p):
         return p // nh, lax.rem(p, nh)
 
-    def owner(head):
-        return lax.rem(head, ns), head // ns
-
-    def map_copies(head):
-        return [
-            pltpu.make_async_remote_copy(
-                src_ref=src.at[head],
-                dst_ref=box.at[me],
-                send_sem=send.at[head],
-                recv_sem=recv.at[me],
-                device_id=owner(head),
-                device_id_type=MESH,
-            )
-            for src, box, send, recv in (
-                (t_out, t_box, t_send, t_recv),
-                (a_out, a_box, a_send, a_recv),
-            )
-        ]
-
-    def state_copy(d):
+    def head_of(group, up, j):
+        return group * UNIT + up * way + j
+
+    def slot_of(group, j):
+        index = group * way + j
+        return lax.rem(index, ns), index // ns
+
+    def remote(src, dst, send, recv, where):
         return pltpu.make_async_remote_copy(
-            src_ref=states.at[d],
-            dst_ref=incoming.at[mine],
-            send_sem=s_send.at[d],
-            recv_sem=s_recv.at[mine],
-            device_id=place(d),
+            src_ref=src,
+            dst_ref=dst,
+            send_sem=send,
+            recv_sem=recv,
+            device_id=where,
             device_id_type=MESH,
         )
+
+    def hop(h, up, t_src, a_src):
+        where = (s, z + 1 if up else z - 1)
+        return [
+            remote(t_src.at[h], t_box.at[h], t_send.at[h], t_recv.at[h], where),
+            remote(a_src.at[h], a_box.at[h], a_send.at[h], a_recv.at[h], where),
+        ]
+
+    def to_owner(h, owner, slot):
+        where = (owner, z)
+        return [
+            remote(
+                t_out.at[h], t_line.at[slot, s], t_send.at[h], tl_recv.at[slot, s], where
+            ),
+            remote(
+                a_out.at[h], a_line.at[slot, s], a_send.at[h], al_recv.at[slot, s], where
+            ),
+        ]
+
+    def from_owner(h, slot, line):
+        return remote(
+            s_line.at[slot, line], s_in.at[h], sl_send.at[slot, line], s_recv.at[h], (line, z)
+        )
+
+    def state_hop(h, up, src):
+        where = (s, z - 1 if up else z + 1)
+        return remote(src.at[h], s_in.at[h], s_send.at[h], s_recv.at[h], where)
+
+    def place_of(up):
+        return z if up else nh - 1 - z
+
+    def compose(tick, up):
+        spot = place_of(up)
+        group = tick - spot
+
+        @pl.when((spot > 0) & (group >= 0) & (group < ticks))
+        def _():
+            picked = [head_of(group, up, j) for j in range(way)]
+            for h in picked:
+                landed(t_box, h, t_recv)
+                landed(a_box, h, a_recv)
+
+            @pl.when((spot < nh - 1) | (s < ns - 1))
+            def _():
+                for h in picked:
+                    if up:
+                        both_maps = cat([t_box[h], a_box[h].astype(F32)], 1)
+                        made = both(t_own[h], both_maps)
+                        extra = a_own[h]
+                    else:
+                        both_maps = cat([t_own[h], a_own[h].astype(F32)], 1)
+                        made = both(t_box[h], both_maps)
+                        extra = a_box[h]
+                    t_out[h] = made[:, :width]
+                    a_out[h] = (made[:, width:] + extra.astype(F32)).astype(a_out.dtype)
+
+                @pl.when(spot < nh - 1)
+                def _():
+                    for h in picked:
+                        for copy in hop(h, up, t_out, a_out):
+                            copy.start()
+
+                @pl.when(spot == nh - 1)
+                def _():
+                    for j, h in enumerate(picked):
+                        owner, slot = slot_of(group, j)
+
+                        @pl.when(owner != s)
+                        def _():
+                            for copy in to_owner(h, owner, slot):
+                                copy.start()
+
+                        @pl.when(owner == s)
+                        def _():
+                            pltpu.make_async_copy(
+                                t_out.at[h], t_line.at[slot, s], tl_recv.at[slot, s]
+                            ).start()
+                            pltpu.make_async_copy(
+                                a_out.at[h], a_line.at[slot, s], al_recv.at[slot, s]
+                            ).start()
+
+    def chain(tick):
+        group = tick - nh
+        j = lax.rem(s + ns * ticks * way - group * way, ns)
+
+        @pl.when(at_end & (group >= 0) & (group < ticks) & (j < way))
+        def _():
+            slot = (group * way + j) // ns
+            h = group * UNIT + jnp.where(z == 0, 0, way) + j
+            landed(init_box, slot, i_recv)
+
+            def send(line, state):
+                s_line[slot, line] = state.astype(s_line.dtype)
+
+                @pl.when(line != s)
+                def _():
+                    from_owner(h, slot, line).start()
+
+                @pl.when(line == s)
+                def _():
+                    pltpu.make_async_copy(
+                        s_line.at[slot, line], s_in.at[h], s_recv.at[h]
+                    ).start()
+
+            def advance(line, state):
+                send(line, state)
+                landed(t_line, (slot, line), tl_recv)
+                landed(a_line, (slot, line), al_recv)
+                return both(t_line[slot, line], state) + a_line[slot, line].astype(F32)
+
+            send(ns - 1, lax.fori_loop(0, ns - 1, advance, init_box[slot]))
+
+    def finish(h, state):
+        raw = local[h] + exact_right(gain[h], state)
+        mean = jnp.mean(raw * raw, axis=-1, keepdims=True)
+        out_ref[h] = (raw * lax.rsqrt(mean + 1e-06)).astype(out_ref.dtype)
+
+    def settle(tick, up):
+        spot = place_of(up)
+        group = tick - 2 * nh + spot
+
+        @pl.when((group >= 0) & (group < ticks))
+        def _():
+            picked = [head_of(group, up, j) for j in range(way)]
+            for h in picked:
+                landed(s_in, h, s_recv)
+
+            if up:
+
+                @pl.when(spot > 0)
+                def _():
+                    for h in picked:
+                        state_hop(h, up, s_in).start()
+                    for h in picked:
+                        state = exact_right(t_box[h], s_in[h]) + a_box[h].astype(F32)
+                        finish(h, state.astype(BF16))
+
+                @pl.when(spot == 0)
+                def _():
+                    for h in picked:
+                        finish(h, s_in[h])
+
+            else:
+
+                @pl.when(spot > 0)
+                def _():
+                    for h in picked:
+                        state = exact_right(t_own[h], s_in[h]) + a_own[h].astype(F32)
+                        s_fwd[h] = state.astype(BF16)
+                    for h in picked:
+                        state_hop(h, up, s_fwd).start()
+
+                for h in picked:
+                    finish(h, s_in[h])
+
+    def exchange(tick):
+        for up in (0, 1):
+            compose(tick, up)
+        chain(tick)
+        for up in (0, 1):
+            settle(tick, up)
+
+    own = init_ref.shape[0]
+
+    def init_copies():
+        for i in range(own):
+            h = z * own + i
+            up = (i % UNIT) // way
+            owner, slot = slot_of(h // UNIT, i % way)
+            copy = remote(
+                init_ref.at[i], init_box.at[slot], i_send.at[i], i_recv.at[slot], (s, ends[up])
+            )
+            yield i, up, owner, slot, copy
 
     @pl.when(step == 0)
     def _():
@@ -255,88 +430,97 @@
 
         pl.semaphore_wait(barrier, n - 1)
 
-    first = group_of(step, ns, nh, size) * size
-    pairs = local_maps(q_ref, k_ref, v_ref, local, gain, first)
-    for h, pair in enumerate(pairs):
-        t_out[first + h] = pair[:, width:]
-        a_out[first + h] = pair[:, :width].astype(a_out.dtype)
-
-    @pl.loop(first, first + size)
-    def _(head):
-        @pl.when(head != mine)
-        def _():
-            for copy in map_copies(head):
+        for i, up, owner, slot, copy in init_copies():
+
+            @pl.when((owner == s) & (z != ends[up]))
+            def _():
                 copy.start()
 
-        @pl.when(head == mine)
-        def _():
-            pltpu.make_async_copy(t_out.at[mine], t_box.at[me], t_recv.at[me]).start()
-            pltpu.make_async_copy(a_out.at[mine], a_box.at[me], a_recv.at[me]).start()
+            @pl.when((owner == s) & (z == ends[up]))
+            def _():
+                pltpu.make_async_copy(
+                    init_ref.at[i], init_box.at[slot], i_recv.at[slot]
+                ).start()
+
+    first = step * size
+    for sub in range(size // UNIT):
+        picked = list(range(sub * UNIT, (sub + 1) * UNIT))
+        pairs = local_maps(q_ref, k_ref, v_ref, local, gain, first, picked)
+        for h, pair in zip(picked, pairs):
+            t_own[first + h] = pair[:, width:]
+            a_own[first + h] = pair[:, :width].astype(a_own.dtype)
+        for up in (0, 1):
+
+            @pl.when(place_of(up) == 0)
+            def _():
+                for h in picked[up * way : (up + 1) * way]:
+                    for copy in hop(first + h, up, t_own, a_own):
+                        copy.start()
+
+        exchange(step * (size // UNIT) + sub)
 
     @pl.when(step == pl.num_programs(0) - 1)
     def _():
-        def advance(d, state):
-            states[d] = state.astype(states.dtype)
-
-            @pl.when(d != me)
+        @pl.loop(ticks, ticks + 2 * nh)
+        def _(tick):
+            exchange(tick)
+
+        for i, up, owner, slot, copy in init_copies():
+
+            @pl.when((owner == s) & (z != ends[up]))
             def _():
-                state_copy(d).start()
-
-            @pl.when(d == me)
-            def _():
-                pltpu.make_async_copy(
-                    states.at[d], incoming.at[mine], s_recv.at[mine]
-                ).start()
-
-            pltpu.make_async_copy(t_box.at[d], t_box.at[d], t_recv.at[d]).wait()
-            pltpu.make_async_copy(a_box.at[d], a_box.at[d], a_recv.at[d]).wait()
-            return both(t_box[d], state) + a_box[d].astype(F32)
-
-        lax.fori_loop(0, n, advance, init_ref[si])
-
-        @pl.loop(0, n // size)
-        def _(g):
-            heads = [g * size + h for h in range(size)]
-            for head in heads:
-                pltpu.make_async_copy(
-                    incoming.at[head], incoming.at[head], s_recv.at[head]
-                ).wait()
-            for head in heads:
-                raw = local[head] + exact_right(gain[head], incoming[head])
-                mean = jnp.mean(raw * raw, axis=-1, keepdims=True)
-                out_ref[head] = (raw * lax.rsqrt(mean + 1e-06)).astype(out_ref.dtype)
-
-        @pl.loop(0, n)
-        def _(head):
-            @pl.when(head != mine)
-            def _():
-                for copy in map_copies(head):
-                    copy.wait_send()
-
-            @pl.when(head != me)
-            def _():
-                state_copy(head).wait_send()
+                copy.wait_send()
+
+        @pl.loop(0, ticks)
+        def _(group):
+            for up in (0, 1):
+                spot = place_of(up)
+                for j in range(way):
+                    h = head_of(group, up, j)
+                    owner, slot = slot_of(group, j)
+
+                    @pl.when(spot < nh - 1)
+                    def _():
+                        for copy in hop(h, up, t_out, a_out):
+                            copy.wait_send()
+
+                    @pl.when((spot == nh - 1) & (owner != s) & (s < ns - 1))
+                    def _():
+                        for copy in to_owner(h, owner, slot):
+                            copy.wait_send()
+
+                    @pl.when(spot > 0)
+                    def _():
+                        state_hop(h, up, s_fwd).wait_send()
+
+                    @pl.when((spot == nh - 1) & (owner == s))
+                    def _():
+                        @pl.loop(0, ns)
+                        def _(line):
+                            @pl.when(line != s)
+                            def _():
+                                from_owner(h, slot, line).wait_send()
 
 
 def mixer(q, k, v, initial_state):
     ns, nh = lax.axis_size("seq"), lax.axis_size("head")
     tokens, heads, width = q.shape
     g = HEADS_A_STEP
-
-    def spec(rows):
-        return pl.BlockSpec((g, rows, width), lambda i: (group_of(i, ns, nh, g), 0, 0))
+    slots = heads // (2 * ns)
+    dma = pltpu.SemaphoreType.DMA
 
     def by_token(rows):
-        return pl.BlockSpec(
-            (tokens, g, rows, width), lambda i: (0, group_of(i, ns, nh, g), 0, 0)
-        )
-
-    square = (heads, width, width)
+        return pl.BlockSpec((tokens, g, rows, width), lambda i: (0, i, 0, 0))
+
+    def maps(*lead):
+        square = (*lead, width, width)
+        return [pltpu.VMEM(square, F32), pltpu.VMEM(square, BF16)]
+
     return pl.pallas_call(
         functools.partial(mixer_kernel, ns, nh),
         grid=(heads // g,),
         in_specs=[
-            pl.BlockSpec((tokens, g, width), lambda i: (0, group_of(i, ns, nh, g), 0)),
+            pl.BlockSpec((tokens, g, width), lambda i: (0, i, 0)),
             by_token(k.shape[2]),
             by_token(k.shape[2]),
             pl.BlockSpec(initial_state.shape, lambda i: (0, 0, 0)),
@@ -346,14 +530,26 @@
         scratch_shapes=[
             pltpu.VMEM((heads, tokens, width), F32),
             pltpu.VMEM((heads, tokens, width), F32),
-            pltpu.VMEM(square, F32),
-            pltpu.VMEM(square, BF16),
-            pltpu.VMEM(square, F32),
-            pltpu.VMEM(square, BF16),
-            pltpu.VMEM(square, BF16),
-            pltpu.VMEM(square, BF16),
-        ]
-        + [pltpu.SemaphoreType.DMA((heads,))] * 6,
+            *maps(heads),
+            *maps(heads),
+            *maps(heads),
+            *maps(slots, ns),
+            pltpu.VMEM((slots, ns, width, width), BF16),
+            pltpu.VMEM((heads, width, width), BF16),
+            pltpu.VMEM((heads, width, width), BF16),
+            pltpu.VMEM((slots, width, width), F32),
+            dma((heads,)),
+            dma((heads,)),
+            dma((heads,)),
+            dma((heads,)),
+            dma((slots, ns)),
+            dma((slots, ns)),
+            dma((slots, ns)),
+            dma((heads,)),
+            dma((heads,)),
+            dma((initial_state.shape[0],)),
+            dma((slots,)),
+        ],
         compiler_params=pltpu.CompilerParams(
             collective_id=0, has_side_effects=True, vmem_limit_bytes=VMEM_BYTES
         ),
@@ -483,12 +679,12 @@
         P(("seq", "head"), None, None, None),
         P("head", None, None),
     )
-    devices = mesh.shape["seq"] * mesh.shape["head"]
 
     def chosen(queries, keys, values, initial_state):
-        own_heads, width = initial_state.shape[:2]
-        inbox = devices * 2 * width * width * 4
-        if own_heads == mesh.shape["seq"] and inbox <= INBOX_BYTES:
+        own_heads = initial_state.shape[0]
+        ns, nh = mesh.shape["seq"], mesh.shape["head"]
+        fits = own_heads % HEADS_A_STEP == 0 and own_heads * nh % (2 * ns) == 0
+        if fits and nh > 1:
             return owned_per_device(queries, keys, values, initial_state)
         return per_device(queries, keys, values, initial_state)
 

time: 132 us -> 118 us (0.89)
  the two profiles are of different devices: /device:TPU:7 before, /device:TPU:2 now
where the time goes in v1:
time: 118 us; the launch traced here: 117 us
  Pallas kernels  113 us (96%)
  local copies, waits for them, and re-layouts  4.26 us (4%)
    pallas_call x1, Pallas kernels, mixer(): pl.pallas_call(functools.partial(mixer_kernel, ns, nh), grid=(heads // g,...  113 us
    transpose x1, local copies, waits for them, and re-layouts, owned_per_device(): return jnp.swapaxes(mixer(queries, keys, values, initial_state), 0, 1)  4.26 us

profile of v1, /device:TPU:2, one launch (start us, length us, event | category | flops | bytes accessed | tf_op | source)
XLA Modules:
  0.0 117.4 jit_solution(4467398163366546635)
XLA Ops:
  0.0 113.2 %mixer.1 = bf16[32,256,128]{2,1,0:T(8,128)(2,1)} custom-call(bf16[256,32,128]{2,1,0:T(8,128)(2,1)} %q_ref.1, bf16[256,32,2,128]{3,2,1,0:T(2,128)(2,1)} %k_ref.1, bf16[256,32,2,128]{3,2,1,0:T(2,128)(2,1)} %v_ref.1, f32[8,128,128]{2,1,0:T(8,128)} %init_ref.1), custom_call_target="tpu_custom_call" | custom-call | tf_op jit(solution)/shard_map/mixer/pallas_call | solution.py:519
  113.2 4.3 %copy.5 = bf16[256,32,128]{2,1,0:T(8,128)(2,1)} copy(bf16[256,32,128]{2,0,1:T(8,128)(2,1)} %bitcast.1) | data formatting | bytes 4194304 | tf_op jit(solution)/shard_map/transpose | solution.py:562

commit v2 on v1

--- a/solution.py
+++ b/solution.py
@@ -1,4 +1,5 @@
 import functools
+import itertools
 
 import jax
 import jax.numpy as jnp
@@ -11,6 +12,9 @@
 BASE = 16
 HEADS_A_STEP = 8
 UNIT = 4
+GROUP = 4
+GRAM_SHARE = 0.25
+BASE_SHARE = 1.15
 VMEM_BYTES = 56 << 20
 
 F32 = jnp.float32
@@ -62,118 +66,154 @@
     return cat(parts, 0)
 
 
-def unit_lower_inverses(xs):
-    n = xs[0].shape[0]
+def twice(pair, right_high, right_low):
+    k = right_high.shape[0]
+    return mm(pair, cat([right_high, right_high], 0)) + mm(pair[:, :k], right_low)
+
+
+def grams(q_ref, k_ref, v_ref, picked, kq_ref, v_own, x_ref, m_ref, d_ref, seen_ref):
+    tokens, _, width = q_ref.shape
+    per_token = k_ref.shape[2]
+    step = min(BLOCK, tokens)
+    n = step * per_token
+    row = lax.broadcasted_iota(jnp.int32, (n, n), 0)
+    col = lax.broadcasted_iota(jnp.int32, (n, n), 1)
+    trow = lax.broadcasted_iota(jnp.int32, (step, n), 0)
+    tcol = lax.broadcasted_iota(jnp.int32, (step, n), 1)
+    visible = tcol < (trow + 1) * per_token
+    for b in range(tokens // step):
+        for j, h in enumerate(picked):
+            i = b * len(picked) + j
+            here = slice(b * step, (b + 1) * step)
+            k = k_ref[here, h].reshape(n, width)
+            kq = cat([k, q_ref[here, h]], 0)
+            kq_ref[i] = kq
+            v_own[i] = v_ref[here, h].reshape(n, width)
+            gs = mm(kq, k, ((1,), (1,)))
+            gram = gs[:n]
+            diag = jnp.where(row == col, gram, 0.0)
+            norm = jnp.sum(diag, axis=1, keepdims=True) + 1e-06
+            d_ref[i] = lax.rsqrt(jnp.sum(diag, axis=0, keepdims=True) + 1e-06)
+            d_col = lax.rsqrt(norm)
+            x = jnp.where(col < row, (2.0 * d_col * d_col) * gram, 0.0)
+            x_ref[i] = cat(split(x), 1)
+            seen_ref[i] = cat(split(jnp.where(visible, gs[n:], 0.0)), 1)
+            packed = jnp.where(col[:BASE] < BASE, x[:BASE], 0.0)
+            for s in range(BASE, n, BASE):
+                inside = (col[:BASE] >= s) & (col[:BASE] < s + BASE)
+                packed = jnp.where(inside, x[s : s + BASE], packed)
+            m_ref[i] = packed
+            yield
+
+
+def base_inverses(m_ref):
+    blocks, _, n = m_ref.shape
+    sub = lax.broadcasted_iota(jnp.int32, (BASE, n), 0)
+    lane = lax.broadcasted_iota(jnp.int32, (BASE, n), 1)
+    invs = [jnp.where(sub == lane % BASE, 1.0, 0.0)] * blocks
+    for j in range(BASE - 1):
+        at = lane - lane % BASE + j
+        for i in range(blocks):
+            coef = jnp.take_along_axis(m_ref[i], at, axis=1)
+            invs[i] = invs[i] - coef * invs[i][j : j + 1]
+            if i % GROUP == GROUP - 1:
+                yield
+    for i, inv in enumerate(invs):
+        m_ref[i] = inv
+
+
+def inverses(v_own, x_ref, m_ref, d_ref, near_ref, fed_ref):
+    blocks, n, _ = near_ref.shape
     row = lax.broadcasted_iota(jnp.int32, (n, n), 0)
     col = lax.broadcasted_iota(jnp.int32, (n, n), 1)
     same = row // BASE == col // BASE
-    sub = lax.broadcasted_iota(jnp.int32, (BASE, n), 0)
-    lane = lax.broadcasted_iota(jnp.int32, (BASE, n), 1)
-    packs = []
-    for x in xs:
-        inner = jnp.where(same, x, 0.0)
-        packed = inner[:BASE]
-        for s in range(BASE, n, BASE):
-            packed = packed + inner[s : s + BASE]
-        packs.append(packed)
-    invs = [jnp.where(sub == lane % BASE, 1.0, 0.0) for _ in xs]
-    for j in range(BASE - 1):
-        at = lane - lane % BASE + j
-        coefs = [jnp.take_along_axis(packed, at, axis=1) for packed in packs]
-        invs = [inv - coef * inv[j : j + 1] for inv, coef in zip(invs, coefs)]
-    ms = [jnp.where(same, cat([inv] * (n // BASE), 0), 0.0) for inv in invs]
+    every = range(blocks)
+    ms = [jnp.where(same, cat([m_ref[i]] * (n // BASE), 0), 0.0) for i in every]
     size = BASE
     while size < n:
-        near = col // size == row // size - 1
-        belows = [split(odd_rows(jnp.where(near, x, 0.0), size)) for x in xs]
-        halves = [split(m) for m in ms]
-        ys = [both_split(*below, *half) for below, half in zip(belows, halves)]
-        ys = [split(merge_rows(jnp.zeros((n, n), F32), y, size)) for y in ys]
-        zs = [
-            both_split(odd_rows(mh, size), odd_rows(ml, size), *y)
-            for (mh, ml), y in zip(halves, ys)
-        ]
-        ms = [merge_rows(m, odd_rows(m, size) - z, size) for m, z in zip(ms, zs)]
+        near = odd_rows(col // size - row // size, size) == -1
+        halves, ys = [], []
+        for i in every:
+            halves.append(split(ms[i]))
+            ys.append(twice(odd_rows(x_ref[i], size), *halves[i]))
+            if i % GROUP == GROUP - 1:
+                yield
+        for i in every:
+            y = jnp.where(near, ys[i], 0.0)
+            ys[i] = split(merge_rows(jnp.zeros((n, n), F32), y, size))
+            if i % GROUP == GROUP - 1:
+                yield
+        for i in every:
+            mh, ml = halves[i]
+            z = both_split(odd_rows(mh, size), odd_rows(ml, size), *ys[i])
+            ms[i] = merge_rows(ms[i], odd_rows(ms[i], size) - z, size)
+            if i % GROUP == GROUP - 1:
+                yield
         size *= 2
-    return ms
-
-
-def block_factors(blocks):
-    n, width = blocks[0][1].shape
-    tokens = blocks[0][0].shape[0]
-    row = lax.broadcasted_iota(jnp.int32, (n, n), 0)
-    col = lax.broadcasted_iota(jnp.int32, (n, n), 1)
-    trow = lax.broadcasted_iota(jnp.int32, (tokens, n), 0)
-    tcol = lax.broadcasted_iota(jnp.int32, (tokens, n), 1)
-    visible = tcol < (trow + 1) * (n // tokens)
-    kqs = [cat([k, q], 0) for q, k, _ in blocks]
-    products = [mm(kq, k, ((1,), (1,))) for kq, (_, k, _) in zip(kqs, blocks)]
-    xs, d_cols, d_rows, seens = [], [], [], []
-    for gs in products:
-        gram = gs[:n]
-        diag = jnp.where(row == col, gram, 0.0)
-        d_col = lax.rsqrt(jnp.sum(diag, axis=1, keepdims=True) + 1e-06)
-        d_row = lax.rsqrt(jnp.sum(diag, axis=0, keepdims=True) + 1e-06)
-        xs.append(jnp.where(col < row, (2.0 * d_col) * gram * d_row, 0.0))
-        d_cols.append(d_col)
-        d_rows.append(d_row)
-        seens.append(split(jnp.where(visible, gs[n:], 0.0)))
-    scaled = [m * (2.0 * d_col) for m, d_col in zip(unit_lower_inverses(xs), d_cols)]
-    feds = [exact_right(m, v) for m, (_, _, v) in zip(scaled, blocks)]
-    nears = [split(m * d_row) for m, d_row in zip(scaled, d_rows)]
-    return kqs, nears, feds, seens
-
-
-def local_maps(q_ref, k_ref, v_ref, local_ref, gain_ref, first, picked):
-    tokens, _, width = q_ref.shape
-    heads = len(picked)
-    per_token = k_ref.shape[2]
-    step = min(BLOCK, tokens)
-    n = step * per_token
-    count = tokens // step
-    blocks = [
-        (
-            q_ref[b * step : (b + 1) * step, h],
-            k_ref[b * step : (b + 1) * step, h].reshape(n, width),
-            v_ref[b * step : (b + 1) * step, h].reshape(n, width),
-        )
-        for b in range(count)
-        for h in picked
-    ]
-    kqs, nears, feds, seens = block_factors(blocks)
+    for i in every:
+        d = d_ref[i]
+        fed_ref[i] = exact_right(ms[i] * (2.0 * d), v_own[i])
+        near_ref[i] = cat(split(ms[i] * (2.0 * d * d)), 1)
+        if i % GROUP == GROUP - 1:
+            yield
+
+
+def local_maps(
+    heads, kq_ref, near_ref, fed_ref, seen_ref, local_ref, gain_ref, t_ref, a_ref, first
+):
+    _, rows, width = kq_ref.shape
+    n = near_ref.shape[1]
+    step = rows - n
+    count = kq_ref.shape[0] // heads
     row = lax.broadcasted_iota(jnp.int32, (width, width), 0)
     col = lax.broadcasted_iota(jnp.int32, (width, width), 1)
     eye = jnp.where(row == col, 1.0, 0.0)
     pairs = [cat([jnp.zeros((width, width), F32), eye], 1)] * heads
     for b in range(count):
-        at = slice(b * heads, (b + 1) * heads)
+        at = range(b * heads, (b + 1) * heads)
         if b == 0:
-            qs = [kq[n:].astype(F32) for kq in kqs[at]]
-            passed = [cat([jnp.zeros_like(q), q], 1) for q in qs]
-            feeds = [
-                cat([fed, -mm(cat(list(near), 1), cat([kq[:n], kq[:n]], 0))], 1)
-                for fed, near, kq in zip(feds[at], nears[at], kqs[at])
-            ]
+            passed, feeds = [], []
+            for i in at:
+                kq = kq_ref[i]
+                q = kq[n:].astype(F32)
+                passed.append(cat([jnp.zeros_like(q), q], 1))
+                feeds.append(cat([fed_ref[i], -mm(near_ref[i], cat([kq[:n], kq[:n]], 0))], 1))
+                yield
         else:
-            aheads = [exact_left(kq, pair) for kq, pair in zip(kqs[at], pairs)]
+            aheads = []
+            for i, pair in zip(at, pairs):
+                aheads.append(exact_left(kq_ref[i], pair))
+                yield
             passed = [ahead[n:] for ahead in aheads]
-            feeds = [
-                cat([fed, jnp.zeros_like(fed)], 1) - both_split(*near, *split(ahead[:n]))
-                for fed, near, ahead in zip(feds[at], nears[at], aheads)
-            ]
+            feeds = []
+            for i, ahead in zip(at, aheads):
+                fed = cat([fed_ref[i], jnp.zeros((n, width), F32)], 1)
+                feeds.append(fed - twice(near_ref[i], *split(ahead[:n])))
+                yield
         feeds = [split(feed) for feed in feeds]
-        pairs = [
-            pair + mm(cat([kq[:n], kq[:n]], 0), cat(list(feed), 0), ((0,), (0,)))
-            for pair, kq, feed in zip(pairs, kqs[at], feeds)
-        ]
-        outs = [
-            base + both_split(*seen, *feed)
-            for base, seen, feed in zip(passed, seens[at], feeds)
-        ]
-        for h, out in zip(picked, outs):
+        made = []
+        for i, pair, feed in zip(at, pairs, feeds):
+            k = kq_ref[i, :n]
+            made.append(pair + mm(cat([k, k], 0), cat(list(feed), 0), ((0,), (0,))))
+            yield
+        pairs = made
+        for h, (i, base, feed) in enumerate(zip(at, passed, feeds)):
+            out = base + twice(seen_ref[i], *feed)
             local_ref[first + h, b * step : (b + 1) * step] = out[:, :width]
             gain_ref[first + h, b * step : (b + 1) * step] = out[:, width:]
-    return pairs
+            yield
+    for h, pair in enumerate(pairs):
+        t_ref[first + h] = pair[:, width:]
+        a_ref[first + h] = pair[:, :width].astype(a_ref.dtype)
+
+
+def weave(mains, sides, share):
+    owed = 0.0
+    for _ in mains:
+        owed += share
+        while owed >= 1.0:
+            owed -= 1.0
+            next(sides, None)
 
 
 def landed(ref, at, sem):
@@ -213,6 +253,7 @@
     s_recv,
     i_send,
     i_recv,
+    *stages,
 ):
     size, width = q_ref.shape[1], q_ref.shape[2]
     heads = out_ref.shape[0]
@@ -233,7 +274,9 @@
 
     def slot_of(group, j):
         index = group * way + j
-        return lax.rem(index, ns), index // ns
+        turn = lax.rem(index, ns)
+        half = turn // 2
+        return jnp.where(lax.rem(turn, 2) == 0, half, ns - 1 - half), index // ns
 
     def remote(src, dst, send, recv, where):
         return pltpu.make_async_remote_copy(
@@ -281,53 +324,49 @@
 
         @pl.when((spot > 0) & (group >= 0) & (group < ticks))
         def _():
-            picked = [head_of(group, up, j) for j in range(way)]
-            for h in picked:
-                landed(t_box, h, t_recv)
-                landed(a_box, h, a_recv)
-
-            @pl.when((spot < nh - 1) | (s < ns - 1))
+            for j in range(way):
+                join(group, up, j, spot)
+
+    def join(group, up, j, spot):
+        h = head_of(group, up, j)
+        landed(t_box, h, t_recv)
+        landed(a_box, h, a_recv)
+
+        @pl.when((spot < nh - 1) | (s < ns - 1))
+        def _():
+            if up:
+                later_t, later_a, sooner_t, sooner_a = t_own, a_own, t_box, a_box
+            else:
+                later_t, later_a, sooner_t, sooner_a = t_box, a_box, t_own, a_own
+            made = both(later_t[h], cat([sooner_t[h], sooner_a[h].astype(F32)], 1))
+            t_out[h] = made[:, :width]
+            a_out[h] = (made[:, width:] + later_a[h].astype(F32)).astype(a_out.dtype)
+
+            @pl.when(spot < nh - 1)
             def _():
-                for h in picked:
-                    if up:
-                        both_maps = cat([t_box[h], a_box[h].astype(F32)], 1)
-                        made = both(t_own[h], both_maps)
-                        extra = a_own[h]
-                    else:
-                        both_maps = cat([t_own[h], a_own[h].astype(F32)], 1)
-                        made = both(t_box[h], both_maps)
-                        extra = a_box[h]
-                    t_out[h] = made[:, :width]
-                    a_out[h] = (made[:, width:] + extra.astype(F32)).astype(a_out.dtype)
-
-                @pl.when(spot < nh - 1)
-                def _():
-                    for h in picked:
-                        for copy in hop(h, up, t_out, a_out):
-                            copy.start()
-
-                @pl.when(spot == nh - 1)
-                def _():
-                    for j, h in enumerate(picked):
-                        owner, slot = slot_of(group, j)
-
-                        @pl.when(owner != s)
-                        def _():
-                            for copy in to_owner(h, owner, slot):
-                                copy.start()
-
-                        @pl.when(owner == s)
-                        def _():
-                            pltpu.make_async_copy(
-                                t_out.at[h], t_line.at[slot, s], tl_recv.at[slot, s]
-                            ).start()
-                            pltpu.make_async_copy(
-                                a_out.at[h], a_line.at[slot, s], al_recv.at[slot, s]
-                            ).start()
+                for copy in hop(h, up, t_out, a_out):
+                    copy.start()
+
+            owner, slot = slot_of(group, j)
+
+            @pl.when((spot == nh - 1) & (owner != s))
+            def _():
+                for copy in to_owner(h, owner, slot):
+                    copy.start()
+
+            @pl.when((spot == nh - 1) & (owner == s))
+            def _():
+                pltpu.make_async_copy(
+                    t_out.at[h], t_line.at[slot, s], tl_recv.at[slot, s]
+                ).start()
+                pltpu.make_async_copy(
+                    a_out.at[h], a_line.at[slot, s], al_recv.at[slot, s]
+                ).start()
 
     def chain(tick):
         group = tick - nh
-        j = lax.rem(s + ns * ticks * way - group * way, ns)
+        turn = jnp.where(s < ns // 2, 2 * s, 2 * (ns - 1 - s) + 1)
+        j = lax.rem(turn + ns * ticks * way - group * way, ns)
 
         @pl.when(at_end & (group >= 0) & (group < ticks) & (j < way))
         def _():
@@ -354,10 +393,10 @@
                 landed(a_line, (slot, line), al_recv)
                 return both(t_line[slot, line], state) + a_line[slot, line].astype(F32)
 
-            send(ns - 1, lax.fori_loop(0, ns - 1, advance, init_box[slot]))
-
-    def finish(h, state):
-        raw = local[h] + exact_right(gain[h], state)
+            send(ns - 1, lax.fori_loop(0, ns - 1, advance, init_box[slot], unroll=True))
+
+    def finish(h, read):
+        raw = local[h] + read
         mean = jnp.mean(raw * raw, axis=-1, keepdims=True)
         out_ref[h] = (raw * lax.rsqrt(mean + 1e-06)).astype(out_ref.dtype)
 
@@ -368,36 +407,37 @@
         @pl.when((group >= 0) & (group < ticks))
         def _():
             picked = [head_of(group, up, j) for j in range(way)]
-            for h in picked:
-                landed(s_in, h, s_recv)
-
             if up:
 
                 @pl.when(spot > 0)
                 def _():
                     for h in picked:
+                        landed(s_in, h, s_recv)
                         state_hop(h, up, s_in).start()
                     for h in picked:
                         state = exact_right(t_box[h], s_in[h]) + a_box[h].astype(F32)
-                        finish(h, state.astype(BF16))
+                        finish(h, both(gain[h], state))
 
                 @pl.when(spot == 0)
                 def _():
                     for h in picked:
-                        finish(h, s_in[h])
+                        landed(s_in, h, s_recv)
+                    for h in picked:
+                        finish(h, exact_right(gain[h], s_in[h]))
 
             else:
+                for h in picked:
+                    landed(s_in, h, s_recv)
 
                 @pl.when(spot > 0)
                 def _():
                     for h in picked:
                         state = exact_right(t_own[h], s_in[h]) + a_own[h].astype(F32)
                         s_fwd[h] = state.astype(BF16)
-                    for h in picked:
                         state_hop(h, up, s_fwd).start()
 
                 for h in picked:
-                    finish(h, s_in[h])
+                    finish(h, exact_right(gain[h], s_in[h]))
 
     def exchange(tick):
         for up in (0, 1):
@@ -428,8 +468,49 @@
                 barrier, inc=1, device_id=place(lax.rem(me + i, n)), device_id_type=MESH
             )
 
-        pl.semaphore_wait(barrier, n - 1)
-
+    subs = size // UNIT
+    kept = len(stages) // subs
+
+    def stage_of(sub):
+        return stages[sub * kept : (sub + 1) * kept]
+
+    def picked_of(sub):
+        return list(range(sub * UNIT, (sub + 1) * UNIT))
+
+    def advance_maps(done, first, later):
+        none = iter(())
+        invert, carry, gram, base = none, none, none, none
+        if done is not None:
+            kq, near, fed, seen, v_own, x, m, d = stage_of(done)
+            invert = inverses(v_own, x, m, d, near, fed)
+            carry = local_maps(
+                UNIT, kq, near, fed, seen, local, gain, t_own, a_own, first
+            )
+        if later is not None:
+            kq, near, fed, seen, v_own, x, m, d = stage_of(later)
+            gram = grams(
+                q_ref, k_ref, v_ref, picked_of(later), kq, v_own, x, m, d, seen
+            )
+            base = base_inverses(m)
+        sides = itertools.chain(gram, base)
+        weave(invert, sides, GRAM_SHARE)
+        weave(carry, sides, BASE_SHARE)
+        for _ in sides:
+            pass
+
+    def offer(first):
+        for up in (0, 1):
+
+            @pl.when(place_of(up) == 0)
+            def _():
+                for j in range(way):
+                    for copy in hop(first + up * way + j, up, t_own, a_own):
+                        copy.start()
+
+    @pl.when(step == 0)
+    def _():
+        advance_maps(None, None, 0)
+        pl.semaphore_wait(pltpu.get_barrier_semaphore(), n - 1)
         for i, up, owner, slot, copy in init_copies():
 
             @pl.when((owner == s) & (z != ends[up]))
@@ -442,26 +523,23 @@
                     init_ref.at[i], init_box.at[slot], i_recv.at[slot]
                 ).start()
 
-    first = step * size
-    for sub in range(size // UNIT):
-        picked = list(range(sub * UNIT, (sub + 1) * UNIT))
-        pairs = local_maps(q_ref, k_ref, v_ref, local, gain, first, picked)
-        for h, pair in zip(picked, pairs):
-            t_own[first + h] = pair[:, width:]
-            a_own[first + h] = pair[:, :width].astype(a_own.dtype)
-        for up in (0, 1):
-
-            @pl.when(place_of(up) == 0)
-            def _():
-                for h in picked[up * way : (up + 1) * way]:
-                    for copy in hop(first + h, up, t_own, a_own):
-                        copy.start()
-
-        exchange(step * (size // UNIT) + sub)
+    @pl.when(step > 0)
+    def _():
+        advance_maps(subs - 1, step * size - UNIT, 0)
+        offer(step * size - UNIT)
+        exchange(step * subs - 1)
+
+    for sub in range(1, subs):
+        advance_maps(sub - 1, step * size + (sub - 1) * UNIT, sub)
+        offer(step * size + (sub - 1) * UNIT)
+        exchange(step * subs + sub - 1)
 
     @pl.when(step == pl.num_programs(0) - 1)
     def _():
-        @pl.loop(ticks, ticks + 2 * nh)
+        advance_maps(subs - 1, heads - UNIT, None)
+        offer(heads - UNIT)
+
+        @pl.loop(ticks - 1, ticks + 2 * nh)
         def _(tick):
             exchange(tick)
 
@@ -516,6 +594,19 @@
         square = (*lead, width, width)
         return [pltpu.VMEM(square, F32), pltpu.VMEM(square, BF16)]
 
+    step = min(BLOCK, tokens)
+    n = step * k.shape[2]
+    blocks = UNIT * (tokens // step)
+    stage = [
+        pltpu.VMEM((blocks, n + step, width), BF16),
+        pltpu.VMEM((blocks, n, 2 * n), BF16),
+        pltpu.VMEM((blocks, n, width), F32),
+        pltpu.VMEM((blocks, step, 2 * n), BF16),
+        pltpu.VMEM((blocks, n, width), BF16),
+        pltpu.VMEM((blocks, n, 2 * n), BF16),
+        pltpu.VMEM((blocks, BASE, n), F32),
+        pltpu.VMEM((blocks, 1, n), F32),
+    ]
     return pl.pallas_call(
         functools.partial(mixer_kernel, ns, nh),
         grid=(heads // g,),
@@ -549,6 +640,7 @@
             dma((heads,)),
             dma((initial_state.shape[0],)),
             dma((slots,)),
+            *stage * (g // UNIT),
         ],
         compiler_params=pltpu.CompilerParams(
             collective_id=0, has_side_effects=True, vmem_limit_bytes=VMEM_BYTES

time: 118 us -> 104 us (0.88)
  the two profiles are of different devices: /device:TPU:2 before, /device:TPU:4 now
where the time goes in v2:
time: 104 us
  Pallas kernels  99.4 us (96%)
  local copies, waits for them, and re-layouts  4.26 us (4%)
    pallas_call x1, Pallas kernels, mixer(): pl.pallas_call(functools.partial(mixer_kernel, ns, nh), grid=(heads // g,...  99.4 us
    transpose x1, local copies, waits for them, and re-layouts, owned_per_device(): return jnp.swapaxes(mixer(queries, keys, values, initial_state), 0, 1)  4.26 us

profile of v2, /device:TPU:4, one launch (start us, length us, event | category | flops | bytes accessed | tf_op | source)
XLA Modules:
  0.0 103.6 jit_solution(1321990382399450688)
XLA Ops:
  0.0 99.4 %mixer.1 = bf16[32,256,128]{2,1,0:T(8,128)(2,1)} custom-call(bf16[256,32,128]{2,1,0:T(8,128)(2,1)} %q_ref.1, bf16[256,32,2,128]{3,2,1,0:T(2,128)(2,1)} %k_ref.1, bf16[256,32,2,128]{3,2,1,0:T(2,128)(2,1)} %v_ref.1, f32[8,128,128]{2,1,0:T(8,128)} %init_ref.1), custom_call_target="tpu_custom_call" | custom-call | tf_op jit(solution)/shard_map/mixer/pallas_call | solution.py:610
  99.4 4.3 %copy.5 = bf16[256,32,128]{2,1,0:T(8,128)(2,1)} copy(bf16[256,32,128]{2,0,1:T(8,128)(2,1)} %bitcast.1) | data formatting | bytes 4194304 | tf_op jit(solution)/shard_map/transpose | solution.py:654

commit v3 on v2

--- a/solution.py
+++ b/solution.py
@@ -318,43 +318,42 @@
     def place_of(up):
         return z if up else nh - 1 - z
 
-    def compose(tick, up):
+    def group_at(tick, up):
         spot = place_of(up)
         group = tick - spot
-
-        @pl.when((spot > 0) & (group >= 0) & (group < ticks))
-        def _():
-            for j in range(way):
-                join(group, up, j, spot)
-
-    def join(group, up, j, spot):
-        h = head_of(group, up, j)
-        landed(t_box, h, t_recv)
-        landed(a_box, h, a_recv)
-
-        @pl.when((spot < nh - 1) | (s < ns - 1))
-        def _():
+        return group, (spot > 0) & (group >= 0) & (group < ticks)
+
+    def join(todo):
+        places = [(head_of(group, up, j), up, group, j) for group, up, j in todo]
+        for h, *_ in places:
+            landed(t_box, h, t_recv)
+            landed(a_box, h, a_recv)
+        for h, up, _, _ in places:
             if up:
                 later_t, later_a, sooner_t, sooner_a = t_own, a_own, t_box, a_box
             else:
                 later_t, later_a, sooner_t, sooner_a = t_box, a_box, t_own, a_own
-            made = both(later_t[h], cat([sooner_t[h], sooner_a[h].astype(F32)], 1))
-            t_out[h] = made[:, :width]
+            high, low = split(later_t[h])
+            right_high, right_low = split(sooner_t[h])
+            right = cat([right_high, sooner_a[h]], 1)
+            made = mm(cat([high, low], 1), cat([right, right], 0))
+            t_out[h] = made[:, :width] + mm(high, right_low)
             a_out[h] = (made[:, width:] + later_a[h].astype(F32)).astype(a_out.dtype)
+        for h, up, group, j in places:
+            spot = place_of(up)
+            owner, slot = slot_of(group, j)
 
             @pl.when(spot < nh - 1)
             def _():
                 for copy in hop(h, up, t_out, a_out):
                     copy.start()
 
-            owner, slot = slot_of(group, j)
-
-            @pl.when((spot == nh - 1) & (owner != s))
+            @pl.when((spot == nh - 1) & (owner != s) & (s < ns - 1))
             def _():
                 for copy in to_owner(h, owner, slot):
                     copy.start()
 
-            @pl.when((spot == nh - 1) & (owner == s))
+            @pl.when((spot == nh - 1) & (owner == s) & (s < ns - 1))
             def _():
                 pltpu.make_async_copy(
                     t_out.at[h], t_line.at[slot, s], tl_recv.at[slot, s]
@@ -362,6 +361,30 @@
                 pltpu.make_async_copy(
                     a_out.at[h], a_line.at[slot, s], al_recv.at[slot, s]
                 ).start()
+
+    def compose(tick):
+        (down, down_on), (raised, up_on) = group_at(tick, 0), group_at(tick, 1)
+
+        @pl.when(down_on & up_on)
+        def _():
+            join([(raised, 1, j) for j in range(way)] + [(down, 0, j) for j in range(way)])
+
+        @pl.when(down_on & ~up_on)
+        def _():
+            join([(down, 0, j) for j in range(way)])
+
+        @pl.when(up_on & ~down_on)
+        def _():
+            join([(raised, 1, j) for j in range(way)])
+
+    def compose_singly(tick):
+        for j in range(way):
+            for up in (1, 0):
+                group, on = group_at(tick, up)
+
+                @pl.when(on)
+                def _():
+                    join([(group, up, j)])
 
     def chain(tick):
         group = tick - nh
@@ -439,9 +462,8 @@
                 for h in picked:
                     finish(h, exact_right(gain[h], s_in[h]))
 
-    def exchange(tick):
-        for up in (0, 1):
-            compose(tick, up)
+    def exchange(tick, pieces=compose):
+        pieces(tick)
         chain(tick)
         for up in (0, 1):
             settle(tick, up)
@@ -541,7 +563,7 @@
 
         @pl.loop(ticks - 1, ticks + 2 * nh)
         def _(tick):
-            exchange(tick)
+            exchange(tick, compose_singly)
 
         for i, up, owner, slot, copy in init_copies():
 

time: 104 us -> 102 us (0.981)
  Pallas kernels: 99.4 us -> 97.2 us
    pallas_call x1, Pallas kernels: 99.4 us -> 97.2 us  [mixer(): pl.pallas_call(functools.partial(mixer_kernel, ns, nh), grid=(heads // g,...]
where the time goes in v3:
time: 102 us
  Pallas kernels  97.2 us (95%)
  local copies, waits for them, and re-layouts  4.26 us (4%)
    pallas_call x1, Pallas kernels, mixer(): pl.pallas_call(functools.partial(mixer_kernel, ns, nh), grid=(heads // g,...  97.2 us
    transpose x1, local copies, waits for them, and re-layouts, owned_per_device(): return jnp.swapaxes(mixer(queries, keys, values, initial_state), 0, 1)  4.26 us

profile of v3, /device:TPU:4, one launch (start us, length us, event | category | flops | bytes accessed | tf_op | source)
XLA Modules:
  0.0 101.5 jit_solution(15845294110179921447)
XLA Ops:
  0.0 97.2 %mixer.1 = bf16[32,256,128]{2,1,0:T(8,128)(2,1)} custom-call(bf16[256,32,128]{2,1,0:T(8,128)(2,1)} %q_ref.1, bf16[256,32,2,128]{3,2,1,0:T(2,128)(2,1)} %k_ref.1, bf16[256,32,2,128]{3,2,1,0:T(2,128)(2,1)} %v_ref.1, f32[8,128,128]{2,1,0:T(8,128)} %init_ref.1), custom_call_target="tpu_custom_call" | custom-call | tf_op jit(solution)/shard_map/mixer/pallas_call | solution.py:632
  97.3 4.3 %copy.5 = bf16[256,32,128]{2,1,0:T(8,128)(2,1)} copy(bf16[256,32,128]{2,0,1:T(8,128)(2,1)} %bitcast.1) | data formatting | bytes 4194304 | tf_op jit(solution)/shard_map/transpose | solution.py:676

commit v4 on v3

--- a/solution.py
+++ b/solution.py
@@ -71,8 +71,8 @@
     return mm(pair, cat([right_high, right_high], 0)) + mm(pair[:, :k], right_low)
 
 
-def grams(q_ref, k_ref, v_ref, picked, kq_ref, v_own, x_ref, m_ref, d_ref, seen_ref):
-    tokens, _, width = q_ref.shape
+def grams(q_ref, k_ref, v_ref, q_rows, picked, kq_ref, v_own, x_ref, m_ref, d_ref, seen_ref):
+    tokens, size, width = q_ref.shape
     per_token = k_ref.shape[2]
     step = min(BLOCK, tokens)
     n = step * per_token
@@ -82,11 +82,15 @@
     tcol = lax.broadcasted_iota(jnp.int32, (step, n), 1)
     visible = tcol < (trow + 1) * per_token
     for b in range(tokens // step):
+        if picked[0] == 0:
+            q = q_ref[b * step : (b + 1) * step].astype(F32)
+            q_rows[b * step * size : (b + 1) * step * size] = q.reshape(-1, width)
         for j, h in enumerate(picked):
             i = b * len(picked) + j
             here = slice(b * step, (b + 1) * step)
             k = k_ref[here, h].reshape(n, width)
-            kq = cat([k, q_ref[here, h]], 0)
+            q = q_rows[pl.ds(b * step * size + h, step, stride=size)]
+            kq = cat([k, q.astype(BF16)], 0)
             kq_ref[i] = kq
             v_own[i] = v_ref[here, h].reshape(n, width)
             gs = mm(kq, k, ((1,), (1,)))
@@ -253,6 +257,7 @@
     s_recv,
     i_send,
     i_recv,
+    q_rows,
     *stages,
 ):
     size, width = q_ref.shape[1], q_ref.shape[2]
@@ -423,49 +428,51 @@
         mean = jnp.mean(raw * raw, axis=-1, keepdims=True)
         out_ref[h] = (raw * lax.rsqrt(mean + 1e-06)).astype(out_ref.dtype)
 
-    def settle(tick, up):
-        spot = place_of(up)
-        group = tick - 2 * nh + spot
-
-        @pl.when((group >= 0) & (group < ticks))
+    def settled_at(tick, up):
+        group = tick - 2 * nh + place_of(up)
+        return [head_of(group, up, j) for j in range(way)], (group >= 0) & (group < ticks)
+
+    def relay(tick, up):
+        picked, on = settled_at(tick, up)
+
+        @pl.when(on)
         def _():
-            picked = [head_of(group, up, j) for j in range(way)]
-            if up:
-
-                @pl.when(spot > 0)
-                def _():
-                    for h in picked:
-                        landed(s_in, h, s_recv)
+            for h in picked:
+                landed(s_in, h, s_recv)
+
+            @pl.when(place_of(up) > 0)
+            def _():
+                for h in picked:
+                    if up:
                         state_hop(h, up, s_in).start()
-                    for h in picked:
-                        state = exact_right(t_box[h], s_in[h]) + a_box[h].astype(F32)
-                        finish(h, both(gain[h], state))
-
-                @pl.when(spot == 0)
-                def _():
-                    for h in picked:
-                        landed(s_in, h, s_recv)
-                    for h in picked:
-                        finish(h, exact_right(gain[h], s_in[h]))
-
-            else:
-                for h in picked:
-                    landed(s_in, h, s_recv)
-
-                @pl.when(spot > 0)
-                def _():
-                    for h in picked:
+                    else:
                         state = exact_right(t_own[h], s_in[h]) + a_own[h].astype(F32)
                         s_fwd[h] = state.astype(BF16)
                         state_hop(h, up, s_fwd).start()
 
+    def settle(tick, up):
+        picked, on = settled_at(tick, up)
+        moved = (place_of(up) > 0) if up else False
+
+        if up:
+
+            @pl.when(on & moved)
+            def _():
                 for h in picked:
-                    finish(h, exact_right(gain[h], s_in[h]))
+                    state = exact_right(t_box[h], s_in[h]) + a_box[h].astype(F32)
+                    finish(h, both(gain[h], state))
+
+        @pl.when(on & ~moved if up else on)
+        def _():
+            for h in picked:
+                finish(h, exact_right(gain[h], s_in[h]))
 
     def exchange(tick, pieces=compose):
         pieces(tick)
         chain(tick)
-        for up in (0, 1):
+        for up in (1, 0):
+            relay(tick, up)
+        for up in (1, 0):
             settle(tick, up)
 
     own = init_ref.shape[0]
@@ -511,7 +518,7 @@
         if later is not None:
             kq, near, fed, seen, v_own, x, m, d = stage_of(later)
             gram = grams(
-                q_ref, k_ref, v_ref, picked_of(later), kq, v_own, x, m, d, seen
+                q_ref, k_ref, v_ref, q_rows, picked_of(later), kq, v_own, x, m, d, seen
             )
             base = base_inverses(m)
         sides = itertools.chain(gram, base)
@@ -662,6 +669,7 @@
             dma((heads,)),
             dma((initial_state.shape[0],)),
             dma((slots,)),
+            pltpu.VMEM((tokens * g, width), F32),
             *stage * (g // UNIT),
         ],
         compiler_params=pltpu.CompilerParams(

time: 102 us -> 98.8 us (0.969)
  Pallas kernels: 97.2 us -> 93.7 us
    pallas_call x1, Pallas kernels: 97.2 us -> 93.7 us  [mixer(): pl.pallas_call(functools.partial(mixer_kernel, ns, nh), grid=(heads // g,...]
where the time goes in v4:
time: 98.8 us; the launch traced here: 98 us
  Pallas kernels  93.7 us (95%)
  local copies, waits for them, and re-layouts  4.26 us (4%)
    pallas_call x1, Pallas kernels, mixer(): pl.pallas_call(functools.partial(mixer_kernel, ns, nh), grid=(heads // g,...  93.7 us
    transpose x1, local copies, waits for them, and re-layouts, owned_per_device(): return jnp.swapaxes(mixer(queries, keys, values, initial_state), 0, 1)  4.26 us

profile of v4, /device:TPU:4, one launch (start us, length us, event | category | flops | bytes accessed | tf_op | source)
XLA Modules:
  0.0 98.0 jit_solution(2151713013020129929)
XLA Ops:
  0.0 93.7 %mixer.1 = bf16[32,256,128]{2,1,0:T(8,128)(2,1)} custom-call(bf16[256,32,128]{2,1,0:T(8,128)(2,1)} %q_ref.1, bf16[256,32,2,128]{3,2,1,0:T(2,128)(2,1)} %k_ref.1, bf16[256,32,2,128]{3,2,1,0:T(2,128)(2,1)} %v_ref.1, f32[8,128,128]{2,1,0:T(8,128)} %init_ref.1), custom_call_target="tpu_custom_call" | custom-call | tf_op jit(solution)/shard_map/mixer/pallas_call | solution.py:639
  93.7 4.3 %copy.5 = bf16[256,32,128]{2,1,0:T(8,128)(2,1)} copy(bf16[256,32,128]{2,0,1:T(8,128)(2,1)} %bitcast.1) | data formatting | bytes 4194304 | tf_op jit(solution)/shard_map/transpose | solution.py:684

commit v5 on v4

--- a/solution.py
+++ b/solution.py
@@ -468,8 +468,8 @@
                 finish(h, exact_right(gain[h], s_in[h]))
 
     def exchange(tick, pieces=compose):
+        chain(tick)
         pieces(tick)
-        chain(tick)
         for up in (1, 0):
             relay(tick, up)
         for up in (1, 0):

time: 98.8 us -> 100 us (1.012)
  Pallas kernels: 93.7 us -> 95.2 us
    pallas_call x1, Pallas kernels: 93.7 us -> 95.2 us  [mixer(): pl.pallas_call(functools.partial(mixer_kernel, ns, nh), grid=(heads // g,...]
where the time goes in v5:
time: 100 us; the launch traced here: 99.5 us
  Pallas kernels  95.2 us (95%)
  local copies, waits for them, and re-layouts  4.26 us (4%)
    pallas_call x1, Pallas kernels, mixer(): pl.pallas_call(functools.partial(mixer_kernel, ns, nh), grid=(heads // g,...  95.2 us
    transpose x1, local copies, waits for them, and re-layouts, owned_per_device(): return jnp.swapaxes(mixer(queries, keys, values, initial_state), 0, 1)  4.26 us

profile of v5, /device:TPU:4, one launch (start us, length us, event | category | flops | bytes accessed | tf_op | source)
XLA Modules:
  0.0 99.5 jit_solution(12815473954509652102)
XLA Ops:
  0.0 95.2 %mixer.1 = bf16[32,256,128]{2,1,0:T(8,128)(2,1)} custom-call(bf16[256,32,128]{2,1,0:T(8,128)(2,1)} %q_ref.1, bf16[256,32,2,128]{3,2,1,0:T(2,128)(2,1)} %k_ref.1, bf16[256,32,2,128]{3,2,1,0:T(2,128)(2,1)} %v_ref.1, f32[8,128,128]{2,1,0:T(8,128)} %init_ref.1), custom_call_target="tpu_custom_call" | custom-call | tf_op jit(solution)/shard_map/mixer/pallas_call | solution.py:639
  95.2 4.3 %copy.5 = bf16[256,32,128]{2,1,0:T(8,128)(2,1)} copy(bf16[256,32,128]{2,0,1:T(8,128)(2,1)} %bitcast.1) | data formatting | bytes 4194304 | tf_op jit(solution)/shard_map/transpose | solution.py:684
